TPU v7x, 128 devices: a whole 4x4x4 slice. The times are simulated.
128 devices in a mesh: dom: 128 (over y, x, z, core).
Axes of the slice: x: 4, y: 4, z: 4, core: 2. Of those that a mesh axis runs over, the one named last changes fastest.
Arguments:
- matrix_tiles: bfloat16 [3072, 27, 128, 128], P('dom'), may hold values from -20 to 20, as said below
- tentative: bfloat16 [3072, 6, 128], P('dom'), may hold values from -0.59765625 to 0.59765625
- column_slots: int32 [3072, 27], P('dom'), may hold values from 0 to 87, as said below
- send_list: int32 [128, 4, 16], P('dom'), may hold values from 0 to 23
- column_aggregate: int32 [3072, 27], P('dom'), may hold values from 0 to 1023, as said below
Outputs:
- coarse: float32 [1024, 6, 432], P('dom')
Inputs may be any that keep to these rules, and one draw needn't show every extreme that they name: column_slots[b, 0] is b's own index in its partition; slots below 24 name own blocks, the last 9 slots of a row name received blocks, only from partitions that exist. column_aggregate names the aggregate of the block that the slot refers to; each aggregate is three blocks of one partition, and the aggregates of partition d are d * 8 to d * 8 + 7. matrix_tiles[b, 0, i, i] lies between 2 and 20.
All inputs are finite; a program needn't handle non-finite values.
Results may differ from a plain program's by a relative error of at most 0.0003.
Values may be sent and summed in bfloat16 or wider, within the bound.
A program may use at most 64 MiB of HBM per device.

v0:
```python
import jax
import jax.numpy as jnp
from jax import lax
from jax.sharding import PartitionSpec as P

R = 2


OMEGA = 0.6


def passed_along(x, axis, by):
    count = lax.axis_size(axis)
    pairs = [(i, i + by) for i in range(count) if 0 <= i + by < count]
    return lax.ppermute(x, axis, pairs)


def for_sending(x):
    return jax.tree.map(lambda a: a.astype(jnp.bfloat16) if a.dtype == jnp.float32 else a, x)


def body(matrix_tiles, tentative, column_slots, send_list, column_aggregate):
    row_blocks = matrix_tiles.shape[0]
    mode_count = tentative.shape[1]
    block_width = tentative.shape[2]
    agg_count = row_blocks // 3
    self_index = lax.axis_index("dom")
    offsets = [peer_slot - R if peer_slot < R else peer_slot - R + 1 for peer_slot in range(2 * R)]
    outgoing = tentative[send_list[0]]
    ghosts = jnp.stack(
        [passed_along(outgoing[peer_slot], "dom", offsets[peer_slot]) for peer_slot in range(2 * R)]
    )
    lookup = jnp.concatenate([tentative, ghosts.reshape(-1, mode_count, block_width)], axis=0)
    columns = lookup[column_slots]
    product = jnp.einsum(
        "bsij,bsmj->bsmi", matrix_tiles, columns, preferred_element_type=jnp.float32
    )
    own_modes = tentative.astype(jnp.float32)
    inverse = 1.0 / jnp.diagonal(matrix_tiles[:, 0], axis1=1, axis2=2).astype(jnp.float32)
    span = (2 * R + 1) * agg_count
    window = (4 * R + 1) * agg_count
    row_base = (self_index - R) * agg_count
    relative = column_aggregate - row_base
    member = (relative[:, :, None] == jnp.arange(span, dtype=jnp.int32)[None, None, :]).astype(
        jnp.float32
    )
    grouped = jnp.einsum("bsr,bsmi->brmi", member, product, precision=lax.Precision.HIGHEST)
    left_side = (
        member[:, 0, :, None, None] * own_modes[:, None, :, :]
        - OMEGA * grouped * inverse[:, None, None, :]
    )
    compact = jnp.einsum("brmi,bcni->rmcn", left_side, grouped, precision=lax.Precision.HIGHEST)
    slab_list = []
    for slab in range(2 * R + 1):
        piece = compact[slab * agg_count : (slab + 1) * agg_count]
        slab_list.append(
            jnp.pad(piece, ((0, 0), (0, 0), ((2 * R - slab) * agg_count, slab * agg_count), (0, 0)))
        )
    slab_set = jnp.stack(slab_list)
    summed = slab_set[R]
    for section in range(2 * R):
        summed = summed + passed_along(
            for_sending(slab_set[offsets[section] + R]), "dom", offsets[section]
        )
    return summed.reshape(agg_count, mode_count, window * mode_count)


def solution(mesh):
    placed = (
        P("dom", None, None, None),
        P("dom", None, None),
        P("dom", None),
        P("dom", None, None),
        P("dom", None),
    )
    return jax.shard_map(
        body, mesh=mesh, in_specs=placed, out_specs=P("dom", None, None), check_vma=False
    )
```

profile of v0, /device:TPU:24, one launch (start us, length us, event | category | flops | bytes accessed | tf_op | source)
XLA Modules:
  0.0 76.6 jit_solution(9569888121914301789)
XLA Ops:
  0.0 0.0 slice-start
  0.0 0.8 compare_select_fusion.1
  0.8 0.1 reshape.46
  0.9 1.7 %gather_fusion = bf16[64,6,128]{2,0,1:T(8,128)(2,1)S(1)} fusion(bf16[24,6,128]{2,0,1:T(8,128)(2,1)} %param.6, s32[1024]{0:T(1024)S(1)} %pad_clamp_fusion.1), kind=kCustom, calls=%fused_computation | custom fusion | bytes 196864 | tf_op jit(solution)/shard_map/gather | solution.py:29
  2.6 8.3 %collective-permute-start = (bf16[16,6,128]{2,0,1:T(8,128)(2,1)S(1)}, bf16[16,6,128]{2,0,1:T(8,128)(2,1)S(1)}, u32[]{:S(2)}, u32[]{:S(2)}) collective-permute-start(bf16[16,6,128]{2,0,1:T(8,128)(2,1)S(1)} %get-tuple-element.9), channel_id=1, source_target_pairs={{2,0},{3,1},{4,2},{5,3},{6,4},{7,5},{8,6},{9,7},{10,8},{11,9},{12,... | collective-permute-start | bytes 73736 | tf_op jit(solution)/shard_map/ppermute | solution.py:15
  10.9 1.9 %collective-permute-start.1 = (bf16[16,6,128]{2,0,1:T(8,128)(2,1)S(1)}, bf16[16,6,128]{2,0,1:T(8,128)(2,1)S(1)}, u32[]{:S(2)}, u32[]{:S(2)}) collective-permute-start(bf16[16,6,128]{2,0,1:T(8,128)(2,1)S(1)} %get-tuple-element.11), channel_id=1, source_target_pairs={{1,0},{2,1},{3,2},{4,3},{5,4},{6,5},{7,6},{8,7},{9,8},{10,9},{11,1... | collective-permute-start | bytes 73736 | tf_op jit(solution)/shard_map/ppermute | solution.py:15
  12.8 2.4 %collective-permute-start.2 = (bf16[16,6,128]{2,0,1:T(8,128)(2,1)S(1)}, bf16[16,6,128]{2,0,1:T(8,128)(2,1)S(1)}, u32[]{:S(2)}, u32[]{:S(2)}) collective-permute-start(bf16[16,6,128]{2,0,1:T(8,128)(2,1)S(1)} %get-tuple-element.10), channel_id=1, source_target_pairs={{0,1},{1,2},{2,3},{3,4},{4,5},{5,6},{6,7},{7,8},{8,9},{9,10},{10,1... | collective-permute-start | bytes 73736 | tf_op jit(solution)/shard_map/ppermute | solution.py:15
  15.2 2.6 %collective-permute-start.3 = (bf16[16,6,128]{2,0,1:T(8,128)(2,1)S(1)}, bf16[16,6,128]{2,0,1:T(8,128)(2,1)S(1)}, u32[]{:S(2)}, u32[]{:S(2)}) collective-permute-start(bf16[16,6,128]{2,0,1:T(8,128)(2,1)S(1)} %get-tuple-element.12), channel_id=1, source_target_pairs={{0,2},{1,3},{2,4},{3,5},{4,6},{5,7},{6,8},{7,9},{8,10},{9,11},{10,... | collective-permute-start | bytes 73736 | tf_op jit(solution)/shard_map/ppermute | solution.py:15
  17.9 0.7 compare_select_fusion
  18.6 0.1 reshape.54
  18.7 0.7 broadcast_subtract_fusion
  19.4 0.2 iota_compare_fusion
  19.6 0.0 slice-done
  19.6 0.0 copy-start
  19.6 3.2 %copy.49 = bf16[24,1,128,128]{0,3,2,1:T(8,128)(2,1)} copy(bf16[24,1,128,128]{3,2,1,0:T(8,128)(2,1)S(1)} %slice-done) | data formatting | bytes 1572864
  22.8 1.9 %gather_fusion.2 = bf16[128,24]{1,0:T(8,128)(2,1)S(1)} fusion(bf16[24,128,128]{0,2,1:T(8,128)(2,1)} %bitcast.42, s32[128]{0:T(128)S(1)} %or_bitcast_fusion), kind=kCustom, calls=%fused_computation.2 | custom fusion | bytes 13312 | tf_op jit(solution)/shard_map/jit(diagonal)/gather | solution.py:39
  24.7 0.1 copy.39
  24.9 0.0 copy-done
  24.9 0.0 collective-permute-done
  24.9 0.0 collective-permute-done.1
  24.9 0.0 collective-permute-done.2
  24.9 0.3 collective-permute-done.3
  25.3 0.1 copy.34
  25.4 2.4 %gather_fusion.1 = bf16[648,6,128]{2,1,0:T(8,128)(2,1)S(1)} fusion(bf16[88,6,128]{2,1,0:T(8,128)(2,1)S(1)} %pad_maximum_fusion, s32[1024]{0:T(1024)S(1)} %pad_clamp_fusion), kind=kCustom, calls=%fused_computation.1 | custom fusion | bytes 1993248 | tf_op jit(solution)/shard_map/gather | solution.py:34
  27.8 14.4 %fusion.15 = f32[24,27,6,128]{3,2,1,0:T(8,128)S(1)} fusion(bf16[24,27,6,128]{3,2,1,0:T(8,128)(2,1)S(1)} %bitcast.41, bf16[24,27,128,128]{3,2,1,0:T(8,128)(2,1)} %param.5), kind=kOutput, calls=%fused_computation.27 | convolution fusion | flops 127401984 | bytes 24219648 | tf_op jit(solution)/shard_map/bsij,bsmj->bsmi/dot_general | solution.py:35
  42.2 2.1 %fusion.4 = f32[24,40,6,128]{3,1,2,0:T(8,128)S(1)} fusion(f32[24,27,6,128]{3,2,1,0:T(8,128)S(1)} %fusion.15, s32[24,27]{1,0:T(8,128)S(1)} %broadcast_subtract_fusion), kind=kOutput, calls=%fused_computation.8 | convolution fusion | flops 238904640 | bytes 4942368 | tf_op jit(solution)/shard_map/bsr,bsmi->brmi/dot_general | solution.py:47
  44.3 7.5 %fusion.14 = (bf16[40,6,40,6]{2,0,3,1:T(8,128)(2,1)S(1)}, f32[40,6,40,6]{2,0,3,1:T(8,128)S(1)}) fusion(f32[24,40,6,128]{3,1,2,0:T(8,128)S(1)} %fusion.4, f32[24,128]{1,0:T(8,128)S(1)} %multiply_bitcast_fusion, f32[24,6,128]{2,1,0:T(8,128)S(1)} %copy.31, f32[24,40]{1,0:T(8,128)S(1)} %bitcast.48), kind=kOutput, calls=%fused_computation.26 | convolution fusion | flops 2125635840 | bytes 3384576 | tf_op jit(solution)/shard_map/brmi,bcni->rmcn/dot_general | solution.py:52
  51.7 0.1 fusion.12
  51.8 0.1 pad.25
  51.9 7.2 %collective-permute-start.4 = (bf16[8,6,72,6]{2,0,3,1:T(8,128)(2,1)S(1)}, bf16[8,6,72,6]{2,0,3,1:T(8,128)(2,1)S(1)}, u32[]{:S(2)}, u32[]{:S(2)}) collective-permute-start(bf16[8,6,72,6]{2,0,3,1:T(8,128)(2,1)S(1)} %pad.25), channel_id=1, source_target_pairs={{2,0},{3,1},{4,2},{5,3},{6,4},{7,5},{8,6},{9,7},{10,8},{11,9},{12,... | collective-permute-start | bytes 124424 | tf_op jit(solution)/shard_map/ppermute | solution.py:15
  59.1 0.1 pad.26
  59.2 2.6 %collective-permute-start.5 = (bf16[8,6,72,6]{2,0,3,1:T(8,128)(2,1)S(1)}, bf16[8,6,72,6]{2,0,3,1:T(8,128)(2,1)S(1)}, u32[]{:S(2)}, u32[]{:S(2)}) collective-permute-start(bf16[8,6,72,6]{2,0,3,1:T(8,128)(2,1)S(1)} %pad.26), channel_id=1, source_target_pairs={{1,0},{2,1},{3,2},{4,3},{5,4},{6,5},{7,6},{8,7},{9,8},{10,9},{11,1... | collective-permute-start | bytes 124424 | tf_op jit(solution)/shard_map/ppermute | solution.py:15
  61.8 0.1 pad.27
  61.8 1.9 %collective-permute-start.6 = (bf16[8,6,72,6]{2,0,3,1:T(8,128)(2,1)S(1)}, bf16[8,6,72,6]{2,0,3,1:T(8,128)(2,1)S(1)}, u32[]{:S(2)}, u32[]{:S(2)}) collective-permute-start(bf16[8,6,72,6]{2,0,3,1:T(8,128)(2,1)S(1)} %pad.27), channel_id=1, source_target_pairs={{0,1},{1,2},{2,3},{3,4},{4,5},{5,6},{6,7},{7,8},{8,9},{9,10},{10,1... | collective-permute-start | bytes 124424 | tf_op jit(solution)/shard_map/ppermute | solution.py:15
  63.8 3.1 %collective-permute-start.7 = (bf16[8,6,72,6]{2,0,3,1:T(8,128)(2,1)S(1)}, bf16[8,6,72,6]{2,0,3,1:T(8,128)(2,1)S(1)}, u32[]{:S(2)}, u32[]{:S(2)}) collective-permute-start(bf16[8,6,72,6]{2,0,3,1:T(8,128)(2,1)S(1)} %pad.28), channel_id=1, source_target_pairs={{0,2},{1,3},{2,4},{3,5},{4,6},{5,7},{6,8},{7,9},{8,10},{9,11},{10,... | collective-permute-start | bytes 124424 | tf_op jit(solution)/shard_map/ppermute | solution.py:15
  66.9 0.0 collective-permute-done.4
  66.9 0.0 collective-permute-done.5
  66.9 4.8 %collective-permute-done.6 = bf16[8,6,72,6]{2,0,3,1:T(8,128)(2,1)S(1)} collective-permute-done((bf16[8,6,72,6]{2,0,3,1:T(8,128)(2,1)S(1)}, bf16[8,6,72,6]{2,0,3,1:T(8,128)(2,1)S(1)}, u32[]{:S(2)}, u32[]{:S(2)}) %collective-permute-start.6) | collective-permute-done | bytes 41504 | tf_op jit(solution)/shard_map/ppermute | solution.py:15
  71.7 3.0 %collective-permute-done.7 = bf16[8,6,72,6]{2,0,3,1:T(8,128)(2,1)S(1)} collective-permute-done((bf16[8,6,72,6]{2,0,3,1:T(8,128)(2,1)S(1)}, bf16[8,6,72,6]{2,0,3,1:T(8,128)(2,1)S(1)}, u32[]{:S(2)}, u32[]{:S(2)}) %collective-permute-start.7) | collective-permute-done | bytes 41504 | tf_op jit(solution)/shard_map/ppermute | solution.py:15
  74.8 0.1 convert_add_fusion
  74.9 0.6 copy.42
  75.5 1.2 %reshape.42 = f32[8,6,432]{2,0,1:T(8,128)} reshape(f32[8,6,72,6]{3,2,0,1:T(8,128)S(1)} %copy.42) | data formatting | bytes 165888 | tf_op jit(solution)/shard_map/reshape | solution.py:65
  (13 shorter events, 0.2 us)
Async XLA Ops:
  0.0 19.6 %slice-start = ((bf16[24,27,128,128]{3,2,1,0:T(8,128)(2,1)}), bf16[24,1,128,128]{3,2,1,0:T(8,128)(2,1)S(1)}, s32[]{:S(2)}) async-start(bf16[24,27,128,128]{3,2,1,0:T(8,128)(2,1)} %param.5), calls=%async_computation | async-start | bytes 1572864 | tf_op jit(solution)/shard_map/slice | solution.py:39
  2.6 22.3 %collective-permute-start = (bf16[16,6,128]{2,0,1:T(8,128)(2,1)S(1)}, bf16[16,6,128]{2,0,1:T(8,128)(2,1)S(1)}, u32[]{:S(2)}, u32[]{:S(2)}) collective-permute-start(bf16[16,6,128]{2,0,1:T(8,128)(2,1)S(1)} %get-tuple-element.9), channel_id=1, source_target_pairs={{2,0},{3,1},{4,2},{5,3},{6,4},{7,5},{8,6},{9,7},{10,8},{11,9},{12,... | collective-permute-start | bytes 73736 | tf_op jit(solution)/shard_map/ppermute | solution.py:15
  10.9 14.0 %collective-permute-start.1 = (bf16[16,6,128]{2,0,1:T(8,128)(2,1)S(1)}, bf16[16,6,128]{2,0,1:T(8,128)(2,1)S(1)}, u32[]{:S(2)}, u32[]{:S(2)}) collective-permute-start(bf16[16,6,128]{2,0,1:T(8,128)(2,1)S(1)} %get-tuple-element.11), channel_id=1, source_target_pairs={{1,0},{2,1},{3,2},{4,3},{5,4},{6,5},{7,6},{8,7},{9,8},{10,9},{11,1... | collective-permute-start | bytes 73736 | tf_op jit(solution)/shard_map/ppermute | solution.py:15
  12.8 12.1 %collective-permute-start.2 = (bf16[16,6,128]{2,0,1:T(8,128)(2,1)S(1)}, bf16[16,6,128]{2,0,1:T(8,128)(2,1)S(1)}, u32[]{:S(2)}, u32[]{:S(2)}) collective-permute-start(bf16[16,6,128]{2,0,1:T(8,128)(2,1)S(1)} %get-tuple-element.10), channel_id=1, source_target_pairs={{0,1},{1,2},{2,3},{3,4},{4,5},{5,6},{6,7},{7,8},{8,9},{9,10},{10,1... | collective-permute-start | bytes 73736 | tf_op jit(solution)/shard_map/ppermute | solution.py:15
  15.2 10.0 %collective-permute-start.3 = (bf16[16,6,128]{2,0,1:T(8,128)(2,1)S(1)}, bf16[16,6,128]{2,0,1:T(8,128)(2,1)S(1)}, u32[]{:S(2)}, u32[]{:S(2)}) collective-permute-start(bf16[16,6,128]{2,0,1:T(8,128)(2,1)S(1)} %get-tuple-element.12), channel_id=1, source_target_pairs={{0,2},{1,3},{2,4},{3,5},{4,6},{5,7},{6,8},{7,9},{8,10},{9,11},{10,... | collective-permute-start | bytes 73736 | tf_op jit(solution)/shard_map/ppermute | solution.py:15
  19.6 5.3 %copy-start = (bf16[24,6,128]{2,0,1:T(8,128)(2,1)S(1)}, bf16[24,6,128]{2,0,1:T(8,128)(2,1)}, u32[]{:S(2)}) copy-start(bf16[24,6,128]{2,0,1:T(8,128)(2,1)} %param.6) | copy-start | bytes 110596
  51.9 15.0 %collective-permute-start.4 = (bf16[8,6,72,6]{2,0,3,1:T(8,128)(2,1)S(1)}, bf16[8,6,72,6]{2,0,3,1:T(8,128)(2,1)S(1)}, u32[]{:S(2)}, u32[]{:S(2)}) collective-permute-start(bf16[8,6,72,6]{2,0,3,1:T(8,128)(2,1)S(1)} %pad.25), channel_id=1, source_target_pairs={{2,0},{3,1},{4,2},{5,3},{6,4},{7,5},{8,6},{9,7},{10,8},{11,9},{12,... | collective-permute-start | bytes 124424 | tf_op jit(solution)/shard_map/ppermute | solution.py:15
  59.2 7.8 %collective-permute-start.5 = (bf16[8,6,72,6]{2,0,3,1:T(8,128)(2,1)S(1)}, bf16[8,6,72,6]{2,0,3,1:T(8,128)(2,1)S(1)}, u32[]{:S(2)}, u32[]{:S(2)}) collective-permute-start(bf16[8,6,72,6]{2,0,3,1:T(8,128)(2,1)S(1)} %pad.26), channel_id=1, source_target_pairs={{1,0},{2,1},{3,2},{4,3},{5,4},{6,5},{7,6},{8,7},{9,8},{10,9},{11,1... | collective-permute-start | bytes 124424 | tf_op jit(solution)/shard_map/ppermute | solution.py:15
  61.8 9.9 %collective-permute-start.6 = (bf16[8,6,72,6]{2,0,3,1:T(8,128)(2,1)S(1)}, bf16[8,6,72,6]{2,0,3,1:T(8,128)(2,1)S(1)}, u32[]{:S(2)}, u32[]{:S(2)}) collective-permute-start(bf16[8,6,72,6]{2,0,3,1:T(8,128)(2,1)S(1)} %pad.27), channel_id=1, source_target_pairs={{0,1},{1,2},{2,3},{3,4},{4,5},{5,6},{6,7},{7,8},{8,9},{9,10},{10,1... | collective-permute-start | bytes 124424 | tf_op jit(solution)/shard_map/ppermute | solution.py:15
  63.8 10.9 %collective-permute-start.7 = (bf16[8,6,72,6]{2,0,3,1:T(8,128)(2,1)S(1)}, bf16[8,6,72,6]{2,0,3,1:T(8,128)(2,1)S(1)}, u32[]{:S(2)}, u32[]{:S(2)}) collective-permute-start(bf16[8,6,72,6]{2,0,3,1:T(8,128)(2,1)S(1)} %pad.28), channel_id=1, source_target_pairs={{0,2},{1,3},{2,4},{3,5},{4,6},{5,7},{6,8},{7,9},{8,10},{9,11},{10,... | collective-permute-start | bytes 124424 | tf_op jit(solution)/shard_map/ppermute | solution.py:15
where the time goes:
time: 77.4 us; the launch traced here: 76.6 us
  starting transfers between devices  30 us (39%)
  matrix products  23.9 us (31%)
  local copies, waits for them, and re-layouts  11.7 us (15%)
  waiting for transfers between devices  8.16 us (11%)
  other arithmetic  2.58 us (3%)
    ppermute x8, starting transfers between devices, passed_along(): return lax.ppermute(x, axis, pairs)  30 us
    dot_general x1, matrix products, body(): jnp.einsum('bsij,bsmj->bsmi', matrix_tiles, columns, preferred_element_ty...  14.4 us
    ppermute x8, waiting for transfers between devices, passed_along(): return lax.ppermute(x, axis, pairs)  8.16 us
    dot_general x1, matrix products, body(): jnp.einsum('brmi,bcni->rmcn', left_side, grouped, precision=lax.Precision...  7.46 us
    unnamed x4, local copies, waits for them, and re-layouts  3.22 us
    gather x1, local copies, waits for them, and re-layouts, body(): columns = lookup[column_slots]  2.4 us
    dot_general x1, matrix products, body(): jnp.einsum('bsr,bsmi->brmi', member, product, precision=lax.Precision.HIG...  2.06 us
    gather x2, local copies, waits for them, and re-layouts, body(): jnp.diagonal(matrix_tiles[:, 0], axis1=1, axis2=2).astype(jnp.float32)  2.01 us
  transfers between devices with their start and end apart: 8, of which 3 were waited for; matrix products, arithmetic and copies ran while one was open for 9% of the time, Pallas kernels for 0%

commit v1 on v0

v1 whole, which is shorter than its diff:
```python
import functools

import jax
import jax.numpy as jnp
from jax import lax
from jax.experimental import pallas as pl
from jax.experimental.pallas import tpu as pltpu
from jax.sharding import PartitionSpec as P

OMEGA = 0.6
RB = 24
K = 27
KO = 18
KG = 9
BS = 128
MODES = 6
GH = 16
SLAB = 48
SPAN = 5 * SLAB
OFFSETS = (-2, -1, 1, 2)
NT = (((1,), (1,)), ((), ()))
U_OWN = 4
U_GH = 4
MESH = pl.DeviceIdType.MESH

dot = functools.partial(lax.dot_general, dimension_numbers=NT, preferred_element_type=jnp.float32)


def expand(x, row_agg):
    r2, r4, r6 = (pltpu.roll(x, s, 0) for s in (2, 4, 6))
    i = lax.broadcasted_iota(jnp.int32, (8, BS), 0)
    v = (jnp.where(i < 6, x, r6), jnp.where(i < 4, r6, r4), jnp.where(i < 2, r4, r2))
    agg = jnp.broadcast_to(x[6:7, :], (8, BS))
    rows = [jnp.where(row_agg[8 * k : 8 * k + 8] == agg, v[k % 3], 0.0) for k in range(6)]
    return jnp.concatenate(rows, axis=0).astype(jnp.bfloat16)


def split(x):
    high = x.astype(jnp.bfloat16)
    low = (x - high.astype(jnp.float32)).astype(jnp.bfloat16)
    return high, low


def kernel(
    count,
    a_hbm, t_hbm, slots_hbm, send_hbm, agg_hbm,
    out_ref,
    a_v, t_v, t8, te_own, te_gh, send_t, recv_t, g_own, weight, acc, send_c, recv_c, result,
    slots, send_list, agg,
    a_sem, small_sem, st_sem, rt_sem, sc_sem, rc_sem,
):
    me = lax.axis_index("dom")
    small = [
        pltpu.make_async_copy(src, dst, small_sem.at[i])
        for i, (src, dst) in enumerate(
            ((agg_hbm, agg), (t_hbm, t_v), (send_hbm, send_list), (slots_hbm, slots))
        )
    ]
    for copy in small:
        copy.start()

    def own_copy(b):
        return pltpu.make_async_copy(
            a_hbm.at[b, pl.ds(0, KO)], a_v.at[b, pl.ds(0, KO)], a_sem.at[0, b]
        )

    def ghost_copy(b):
        return pltpu.make_async_copy(
            a_hbm.at[b, pl.ds(KO, KG)], a_v.at[b, pl.ds(KO, KG)], a_sem.at[1, b]
        )

    for b in range(RB):
        own_copy(b).start()
    for b in range(RB):
        ghost_copy(b).start()

    exists = [jnp.logical_and(me - o >= 0, me - o < count) for o in OFFSETS]
    recv_c[...] = jnp.zeros_like(recv_c)
    barrier = pltpu.get_barrier_semaphore()
    for p, o in enumerate(OFFSETS):
        @pl.when(exists[p])
        def _():
            pl.semaphore_signal(barrier, inc=1, device_id=(me - o,), device_id_type=MESH)

    iota = lax.broadcasted_iota(jnp.int32, (SLAB, BS), 0)
    row_agg = lax.shift_right_logical(iota * 43, 8).astype(jnp.float32)

    small[0].wait()
    small[1].wait()
    for m in range(MODES):
        t8[:, m, :] = t_v[m].astype(jnp.float32)
    for b in range(RB):
        own_agg = (agg[b, 0] - me * 8).astype(jnp.float32)
        t8[b, MODES:8, :] = jnp.full((2, BS), own_agg, jnp.float32)
    small[2].wait()
    for p in range(4):
        for g in range(0, GH, 2):
            pair = [t8[send_list[0, p, g + h]] for h in range(2)]
            send_t[p, g * 8 : g * 8 + 16, :] = jnp.concatenate(pair, axis=0).astype(jnp.bfloat16)

    def own_table(b, c):
        te_own[b] = expand(t8[b], row_agg)
        return c

    lax.fori_loop(0, RB, own_table, 0, unroll=4)

    total = sum(e.astype(jnp.int32) for e in exists)
    pl.semaphore_wait(barrier, total)

    def t_copy(p):
        return pltpu.make_async_remote_copy(
            src_ref=send_t.at[p], dst_ref=recv_t.at[p], send_sem=st_sem.at[p], recv_sem=rt_sem.at[p],
            device_id=(me + OFFSETS[p],), device_id_type=MESH,
        )

    for p in range(4):
        @pl.when(exists[3 - p])
        def _():
            t_copy(p).start()

    def zero_table(v, c):
        te_gh[v] = jnp.zeros((4 * SLAB, BS), jnp.bfloat16)
        return c

    lax.fori_loop(0, 4 * GH, zero_table, 0, unroll=4)
    small[3].wait()

    eye = lax.broadcasted_iota(jnp.int32, (BS, BS), 0) == lax.broadcasted_iota(jnp.int32, (BS, BS), 1)

    def own_rows(step, c):
        for u in range(U_OWN):
            b = step * U_OWN + u
            own_copy(b).wait()
            lhs = jnp.concatenate([te_own[slots[b, s]] for s in range(KO)], axis=1)
            rhs = jnp.concatenate([a_v[b, s] for s in range(KO)], axis=1)
            g_own[b] = dot(lhs, rhs)
            diagonal = jnp.sum(
                jnp.where(eye, a_v[b, 0].astype(jnp.float32), 0.0), axis=0, keepdims=True
            )
            weight[b] = jnp.broadcast_to(-OMEGA * (1.0 / diagonal), (8, BS))
        return c

    lax.fori_loop(0, RB // U_OWN, own_rows, 0)

    for p in range(4):
        @pl.when(exists[p])
        def _():
            t_copy(p).wait_recv()

    for p in range(4):
        def ghost_table(g, c):
            x = recv_t[p, pl.ds(pl.multiple_of(g * 16, 16), 16), :].astype(jnp.float32)
            rows = slice((3 - p) * SLAB, (4 - p) * SLAB)
            te_gh[p * GH + 2 * g, rows, :] = expand(x[0:8], row_agg)
            te_gh[p * GH + 2 * g + 1, rows, :] = expand(x[8:16], row_agg)
            return c

        lax.fori_loop(0, GH // 2, ghost_table, 0, unroll=2)

    acc[...] = jnp.zeros_like(acc)

    def ghost_rows(step, c):
        lefts, rights = ([], []), ([], [])
        for u in range(U_GH):
            b = step * U_GH + u
            ghost_copy(b).wait()
            lhs = jnp.concatenate([te_gh[jnp.maximum(slots[b, s] - RB, 0)] for s in range(KO, K)], axis=1)
            rhs = jnp.concatenate([a_v[b, s] for s in range(KO, K)], axis=1)
            ghost = dot(lhs, rhs)
            own = g_own[b]
            w = weight[b, 0:1]
            own_left = te_own[b].astype(jnp.float32) + own * w
            grouped = jnp.concatenate([ghost[: 2 * SLAB], own, ghost[2 * SLAB :]], axis=0)
            left = jnp.concatenate([ghost[: 2 * SLAB] * w, own_left, ghost[2 * SLAB :] * w], axis=0)
            for whole, parts in ((grouped, rights), (left, lefts)):
                high, low = split(whole)
                parts[0].append(high)
                parts[1].append(low)
        lhs = jnp.concatenate(lefts[0] + lefts[0] + lefts[1], axis=1)
        rhs = jnp.concatenate(rights[0] + rights[1] + rights[0], axis=1)
        acc[...] += dot(lhs, rhs)
        return c

    lax.fori_loop(0, RB // U_GH, ghost_rows, 0)

    def c_copy(p):
        return pltpu.make_async_remote_copy(
            src_ref=send_c.at[p], dst_ref=recv_c.at[p], send_sem=sc_sem.at[p], recv_sem=rc_sem.at[p],
            device_id=(me - OFFSETS[p],), device_id_type=MESH,
        )

    for p, o in enumerate(OFFSETS):
        slab = 2 - o
        send_c[p, :, 0:SPAN] = acc[slab * SLAB : (slab + 1) * SLAB, :].astype(jnp.bfloat16)
        send_c[p, :, SPAN:256] = jnp.zeros((SLAB, 256 - SPAN), jnp.bfloat16)
    for p in range(4):
        @pl.when(exists[p])
        def _():
            c_copy(p).start()

    lane = lax.broadcasted_iota(jnp.int32, (SLAB, 256), 1)
    zeros = jnp.zeros((SLAB, 256), jnp.float32)

    def placed(x, by):
        wide = jnp.concatenate([x, zeros], axis=1)
        return wide if by == 0 else pltpu.roll(wide, by, 1)

    g_own[0, :, :] = acc[2 * SLAB : 3 * SLAB, 0:128]
    g_own[1, :, :] = jnp.zeros((SLAB, BS), jnp.float32)
    g_own[1, :, 0 : SPAN - 128] = acc[2 * SLAB : 3 * SLAB, 128:SPAN]
    summed = placed(jnp.concatenate([g_own[0], g_own[1]], axis=1), 2 * SLAB)
    for p, o in enumerate(OFFSETS):
        @pl.when(exists[3 - p])
        def _():
            c_copy(p).wait_recv()
    for p, o in enumerate(OFFSETS):
        summed = summed + placed(recv_c[p].astype(jnp.float32), (o + 2) * SLAB)
    for t in range(4):
        result[t] = summed[:, t * BS : (t + 1) * BS]
    for m in range(MODES):
        for t in range(4):
            size = min(BS, 9 * SLAB - t * BS)
            rows = result[t, pl.ds(m, 8, stride=MODES), :]
            out_ref[m, :, t * BS : t * BS + size] = rows[:, :size]
    for p in range(4):
        @pl.when(exists[3 - p])
        def _():
            t_copy(p).wait_send()

        @pl.when(exists[p])
        def _():
            c_copy(p).wait_send()


def solution(mesh):
    count = mesh.shape["dom"]
    call = pl.pallas_call(
        functools.partial(kernel, count),
        out_shape=jax.ShapeDtypeStruct((MODES, 8, 9 * SLAB), jnp.float32),
        in_specs=[pl.BlockSpec(memory_space=pl.ANY)] * 5,
        out_specs=pl.BlockSpec(memory_space=pltpu.VMEM),
        scratch_shapes=[
            pltpu.VMEM((RB, K, BS, BS), jnp.bfloat16),
            pltpu.VMEM((MODES, RB, BS), jnp.bfloat16),
            pltpu.VMEM((RB, 8, BS), jnp.float32),
            pltpu.VMEM((RB, SLAB, BS), jnp.bfloat16),
            pltpu.VMEM((4 * GH, 4 * SLAB, BS), jnp.bfloat16),
            pltpu.VMEM((4, GH * 8, BS), jnp.bfloat16),
            pltpu.VMEM((4, GH * 8, BS), jnp.bfloat16),
            pltpu.VMEM((RB, SLAB, BS), jnp.float32),
            pltpu.VMEM((RB, 8, BS), jnp.float32),
            pltpu.VMEM((SPAN, SPAN), jnp.float32),
            pltpu.VMEM((4, SLAB, 256), jnp.bfloat16),
            pltpu.VMEM((4, SLAB, 256), jnp.bfloat16),
            pltpu.VMEM((4, SLAB, BS), jnp.float32),
            pltpu.SMEM((RB, K), jnp.int32),
            pltpu.SMEM((1, 4, GH), jnp.int32),
            pltpu.SMEM((RB, K), jnp.int32),
            pltpu.SemaphoreType.DMA((2, RB)),
            pltpu.SemaphoreType.DMA((4,)),
            pltpu.SemaphoreType.DMA((4,)),
            pltpu.SemaphoreType.DMA((4,)),
            pltpu.SemaphoreType.DMA((4,)),
            pltpu.SemaphoreType.DMA((4,)),
        ],
        compiler_params=pltpu.CompilerParams(
            collective_id=0, has_side_effects=True, vmem_limit_bytes=56 << 20
        ),
    )

    def body(matrix_tiles, tentative, column_slots, send_list, column_aggregate):
        by_mode = call(
            matrix_tiles, tentative.transpose(1, 0, 2), column_slots, send_list, column_aggregate
        )
        return by_mode.transpose(1, 0, 2)

    placed = (
        P("dom", None, None, None),
        P("dom", None, None),
        P("dom", None),
        P("dom", None, None),
        P("dom", None),
    )
    return jax.shard_map(
        body, mesh=mesh, in_specs=placed, out_specs=P("dom", None, None), check_vma=False
    )
```

time: 77.4 us -> 39.6 us (0.51)
  Pallas kernels: 0 us -> 38 us
  starting transfers between devices: 30 us -> 0 us
  matrix products: 23.9 us -> 0 us
  local copies, waits for them, and re-layouts: 11.7 us -> 1.54 us
  waiting for transfers between devices: 8.16 us -> 0 us
  other arithmetic: 2.58 us -> 0 us
    pallas_call x0 -> x1, Pallas kernels: none -> 38 us  [body(): call(matrix_tiles, tentative.transpose(1, 0, 2), column_slots, send_list,...]
    ppermute x8 -> x0, starting transfers between devices: 30 us -> none  [passed_along(): return lax.ppermute(x, axis, pairs)]
    dot_general x3 -> x0, matrix products: 23.9 us -> none  [the longest x1 14.4 us: body(): jnp.einsum('bsij,bsmj->bsmi', matrix_tiles, columns, preferred_element_ty...]
    ppermute x8 -> x0, waiting for transfers between devices: 8.16 us -> none  [passed_along(): return lax.ppermute(x, axis, pairs)]
    gather x4 -> x0, local copies, waits for them, and re-layouts: 6.1 us -> none  [the longest x1 2.4 us: body(): columns = lookup[column_slots]]
    unnamed x4 -> x1, local copies, waits for them, and re-layouts: 3.22 us -> 1.54 us
    select_n x2 -> x0, other arithmetic: 1.47 us -> none  [the longest x1 0.76 us: body(): outgoing = tentative[send_list[0]]]
    reshape x2 -> x0, local copies, waits for them, and re-layouts: 1.23 us -> none  [the longest x1 1.16 us: body(): return summed.reshape(agg_count, mode_count, window * mode_count)]
  transfers between devices with their start and end apart: 8 -> 0, of which waited for: 3 -> 0; matrix products, arithmetic and copies ran while one was open for 9% -> 0% of each run, Pallas kernels for 0% -> 0%
where the time goes in v1:
time: 39.6 us; the launch traced here: 39.5 us
  Pallas kernels  38 us (96%)
  local copies, waits for them, and re-layouts  1.54 us (4%)
    pallas_call x1, Pallas kernels, body(): call(matrix_tiles, tentative.transpose(1, 0, 2), column_slots, send_list,...  38 us
    unnamed x1, local copies, waits for them, and re-layouts  1.54 us

profile of v1, /device:TPU:24, one launch (start us, length us, event | category | flops | bytes accessed | tf_op | source)
XLA Modules:
  0.0 39.5 jit_solution(4411444639785012498)
XLA Ops:
  0.0 38.0 %shard_map.55 = f32[6,8,432]{2,1,0:T(8,128)} custom-call(bf16[24,27,128,128]{3,2,1,0:T(8,128)(2,1)} %a_hbm.1, bf16[6,24,128]{2,1,0:T(8,128)(2,1)} %bitcast.3, s32[24,27]{1,0:T(8,128)} %slots_hbm.1, s32[1,4,16]{2,1,0:T(4,128)} %send_hbm.1, s32[24,27]{1,0:T(8,128)} %agg_hbm.1), custom_call_target="tpu_custom_call" | custom-call | tf_op jit(solution)/shard_map/pallas_call | solution.py:272
  38.0 1.5 %copy.7 = f32[8,6,432]{2,0,1:T(8,128)} copy(f32[8,6,432]{2,0,1:T(8,128)} %bitcast.2) | data formatting | bytes 165888

commit v2 on v1

--- a/solution.py
+++ b/solution.py
@@ -20,7 +20,8 @@
 OFFSETS = (-2, -1, 1, 2)
 NT = (((1,), (1,)), ((), ()))
 U_OWN = 4
-U_GH = 4
+U_GH = 8
+STREAMED = 8
 MESH = pl.DeviceIdType.MESH
 
 dot = functools.partial(lax.dot_general, dimension_numbers=NT, preferred_element_type=jnp.float32)
@@ -59,20 +60,14 @@
     for copy in small:
         copy.start()
 
-    def own_copy(b):
-        return pltpu.make_async_copy(
-            a_hbm.at[b, pl.ds(0, KO)], a_v.at[b, pl.ds(0, KO)], a_sem.at[0, b]
-        )
-
-    def ghost_copy(b):
-        return pltpu.make_async_copy(
-            a_hbm.at[b, pl.ds(KO, KG)], a_v.at[b, pl.ds(KO, KG)], a_sem.at[1, b]
-        )
-
-    for b in range(RB):
-        own_copy(b).start()
-    for b in range(RB):
-        ghost_copy(b).start()
+    def own_copy(step):
+        part = (pl.ds(step * U_OWN, U_OWN), pl.ds(0, KO))
+        return pltpu.make_async_copy(a_hbm.at[part], a_v.at[part], a_sem.at[0, step])
+
+    def ghost_copy(step):
+        part = (pl.ds(step * U_GH, U_GH), pl.ds(KO, KG))
+        return pltpu.make_async_copy(a_hbm.at[part], a_v.at[part], a_sem.at[1, step])
+
 
     exists = [jnp.logical_and(me - o >= 0, me - o < count) for o in OFFSETS]
     recv_c[...] = jnp.zeros_like(recv_c)
@@ -82,17 +77,22 @@
         def _():
             pl.semaphore_signal(barrier, inc=1, device_id=(me - o,), device_id_type=MESH)
 
+    own_copy(0).start()
+    for copy in small:
+        copy.wait()
+    for step in range(1, RB // U_OWN):
+        own_copy(step).start()
+    for step in range(RB // U_GH):
+        ghost_copy(step).start()
+
     iota = lax.broadcasted_iota(jnp.int32, (SLAB, BS), 0)
     row_agg = lax.shift_right_logical(iota * 43, 8).astype(jnp.float32)
 
-    small[0].wait()
-    small[1].wait()
     for m in range(MODES):
         t8[:, m, :] = t_v[m].astype(jnp.float32)
     for b in range(RB):
         own_agg = (agg[b, 0] - me * 8).astype(jnp.float32)
         t8[b, MODES:8, :] = jnp.full((2, BS), own_agg, jnp.float32)
-    small[2].wait()
     for p in range(4):
         for g in range(0, GH, 2):
             pair = [t8[send_list[0, p, g + h]] for h in range(2)]
@@ -123,17 +123,19 @@
         return c
 
     lax.fori_loop(0, 4 * GH, zero_table, 0, unroll=4)
-    small[3].wait()
 
     eye = lax.broadcasted_iota(jnp.int32, (BS, BS), 0) == lax.broadcasted_iota(jnp.int32, (BS, BS), 1)
 
     def own_rows(step, c):
+        own_copy(step).wait()
         for u in range(U_OWN):
             b = step * U_OWN + u
-            own_copy(b).wait()
-            lhs = jnp.concatenate([te_own[slots[b, s]] for s in range(KO)], axis=1)
-            rhs = jnp.concatenate([a_v[b, s] for s in range(KO)], axis=1)
-            g_own[b] = dot(lhs, rhs)
+            still, moving = range(KO - STREAMED), range(KO - STREAMED, KO)
+            table, tiles = (
+                [jnp.concatenate([f(s) for s in part], axis=1) for part in (still, moving)]
+                for f in (lambda s: te_own[slots[b, s]], lambda s: a_v[b, s])
+            )
+            g_own[b] = dot(table[0], tiles[0]) + dot(tiles[1], table[1]).T
             diagonal = jnp.sum(
                 jnp.where(eye, a_v[b, 0].astype(jnp.float32), 0.0), axis=0, keepdims=True
             )
@@ -161,9 +163,9 @@
 
     def ghost_rows(step, c):
         lefts, rights = ([], []), ([], [])
+        ghost_copy(step).wait()
         for u in range(U_GH):
             b = step * U_GH + u
-            ghost_copy(b).wait()
             lhs = jnp.concatenate([te_gh[jnp.maximum(slots[b, s] - RB, 0)] for s in range(KO, K)], axis=1)
             rhs = jnp.concatenate([a_v[b, s] for s in range(KO, K)], axis=1)
             ghost = dot(lhs, rhs)
@@ -236,7 +238,7 @@
     count = mesh.shape["dom"]
     call = pl.pallas_call(
         functools.partial(kernel, count),
-        out_shape=jax.ShapeDtypeStruct((MODES, 8, 9 * SLAB), jnp.float32),
+        out_shape=pltpu.VMEM((MODES, 8, 9 * SLAB), jnp.float32),
         in_specs=[pl.BlockSpec(memory_space=pl.ANY)] * 5,
         out_specs=pl.BlockSpec(memory_space=pltpu.VMEM),
         scratch_shapes=[

time: 39.6 us -> 23 us (0.58)
  Pallas kernels: 38 us -> 22.2 us
  local copies, waits for them, and re-layouts: 1.54 us -> 0.64 us
    pallas_call x1, Pallas kernels: 38 us -> 22.2 us  [body(): call(matrix_tiles, tentative.transpose(1, 0, 2), column_slots, send_list,...]
    unnamed x1, local copies, waits for them, and re-layouts: 1.54 us -> 0.64 us
where the time goes in v2:
time: 23 us; the launch traced here: 22.8 us
  Pallas kernels  22.2 us (97%)
  local copies, waits for them, and re-layouts  0.64 us (3%)
    pallas_call x1, Pallas kernels, body(): call(matrix_tiles, tentative.transpose(1, 0, 2), column_slots, send_list,...  22.2 us
    unnamed x1, local copies, waits for them, and re-layouts  0.64 us

profile of v2, /device:TPU:24, one launch (start us, length us, event | category | flops | bytes accessed | tf_op | source)
XLA Modules:
  0.0 22.8 jit_solution(13987125120880026243)
XLA Ops:
  0.0 22.2 %shard_map.55 = f32[6,8,432]{2,1,0:T(8,128)S(1)} custom-call(bf16[24,27,128,128]{3,2,1,0:T(8,128)(2,1)} %a_hbm.1, bf16[6,24,128]{2,1,0:T(8,128)(2,1)} %bitcast.3, s32[24,27]{1,0:T(8,128)} %slots_hbm.1, s32[1,4,16]{2,1,0:T(4,128)} %send_hbm.1, s32[24,27]{1,0:T(8,128)} %agg_hbm.1), custom_call_target="tpu_custom_call" | custom-call | tf_op jit(solution)/shard_map/pallas_call | solution.py:274
  22.2 0.6 %copy.7 = f32[8,6,432]{2,0,1:T(8,128)} copy(f32[8,6,432]{2,0,1:T(8,128)S(1)} %bitcast.2) | data formatting | bytes 165888

commit v3 on v2

--- a/solution.py
+++ b/solution.py
@@ -19,8 +19,17 @@
 SPAN = 5 * SLAB
 OFFSETS = (-2, -1, 1, 2)
 NT = (((1,), (1,)), ((), ()))
-U_OWN = 4
-U_GH = 8
+OWN = slice(2 * SLAB, 3 * SLAB)
+
+
+def groups(*sizes):
+    return [range(sum(sizes[:i]), sum(sizes[: i + 1])) for i in range(len(sizes))]
+
+
+OWN_GROUPS = groups(4, 4, 4, 4, 4, 4)
+GHOST_GROUPS = groups(8, 8, 8)
+ORDER = [("own", 0), ("own", 1), ("own", 2), ("own", 3), ("own", 4), ("own", 5), ("ghost", 0), ("ghost", 1), ("ghost", 2)]
+AHEAD = 2
 STREAMED = 8
 MESH = pl.DeviceIdType.MESH
 
@@ -46,7 +55,7 @@
     count,
     a_hbm, t_hbm, slots_hbm, send_hbm, agg_hbm,
     out_ref,
-    a_v, t_v, t8, te_own, te_gh, send_t, recv_t, g_own, weight, acc, send_c, recv_c, result,
+    a_v, t_v, t8, te_own, te_gh, send_t, recv_t, g_hi, g_lo, l_hi, l_lo, l_gh, weight, acc, send_c, recv_c, result,
     slots, send_list, agg,
     a_sem, small_sem, st_sem, rt_sem, sc_sem, rc_sem,
 ):
@@ -61,11 +70,13 @@
         copy.start()
 
     def own_copy(step):
-        part = (pl.ds(step * U_OWN, U_OWN), pl.ds(0, KO))
+        group = OWN_GROUPS[step]
+        part = (pl.ds(group.start, len(group)), pl.ds(0, KO))
         return pltpu.make_async_copy(a_hbm.at[part], a_v.at[part], a_sem.at[0, step])
 
     def ghost_copy(step):
-        part = (pl.ds(step * U_GH, U_GH), pl.ds(KO, KG))
+        group = GHOST_GROUPS[step]
+        part = (pl.ds(group.start, len(group)), pl.ds(KO, KG))
         return pltpu.make_async_copy(a_hbm.at[part], a_v.at[part], a_sem.at[1, step])
 
 
@@ -77,13 +88,12 @@
         def _():
             pl.semaphore_signal(barrier, inc=1, device_id=(me - o,), device_id_type=MESH)
 
-    own_copy(0).start()
+    for kind, step in ORDER[:AHEAD]:
+        (own_copy if kind == "own" else ghost_copy)(step).start()
     for copy in small:
         copy.wait()
-    for step in range(1, RB // U_OWN):
-        own_copy(step).start()
-    for step in range(RB // U_GH):
-        ghost_copy(step).start()
+    for kind, step in ORDER[AHEAD:]:
+        (own_copy if kind == "own" else ghost_copy)(step).start()
 
     iota = lax.broadcasted_iota(jnp.int32, (SLAB, BS), 0)
     row_agg = lax.shift_right_logical(iota * 43, 8).astype(jnp.float32)
@@ -126,64 +136,72 @@
 
     eye = lax.broadcasted_iota(jnp.int32, (BS, BS), 0) == lax.broadcasted_iota(jnp.int32, (BS, BS), 1)
 
-    def own_rows(step, c):
+    def own_rows(step):
         own_copy(step).wait()
-        for u in range(U_OWN):
-            b = step * U_OWN + u
+        for b in OWN_GROUPS[step]:
             still, moving = range(KO - STREAMED), range(KO - STREAMED, KO)
             table, tiles = (
                 [jnp.concatenate([f(s) for s in part], axis=1) for part in (still, moving)]
                 for f in (lambda s: te_own[slots[b, s]], lambda s: a_v[b, s])
             )
-            g_own[b] = dot(table[0], tiles[0]) + dot(tiles[1], table[1]).T
+            grouped = dot(table[0], tiles[0]) + dot(tiles[1], table[1]).T
             diagonal = jnp.sum(
                 jnp.where(eye, a_v[b, 0].astype(jnp.float32), 0.0), axis=0, keepdims=True
             )
-            weight[b] = jnp.broadcast_to(-OMEGA * (1.0 / diagonal), (8, BS))
-        return c
-
-    lax.fori_loop(0, RB // U_OWN, own_rows, 0)
-
-    for p in range(4):
-        @pl.when(exists[p])
-        def _():
-            t_copy(p).wait_recv()
-
-    for p in range(4):
-        def ghost_table(g, c):
-            x = recv_t[p, pl.ds(pl.multiple_of(g * 16, 16), 16), :].astype(jnp.float32)
-            rows = slice((3 - p) * SLAB, (4 - p) * SLAB)
-            te_gh[p * GH + 2 * g, rows, :] = expand(x[0:8], row_agg)
-            te_gh[p * GH + 2 * g + 1, rows, :] = expand(x[8:16], row_agg)
-            return c
-
-        lax.fori_loop(0, GH // 2, ghost_table, 0, unroll=2)
-
-    acc[...] = jnp.zeros_like(acc)
-
-    def ghost_rows(step, c):
-        lefts, rights = ([], []), ([], [])
+            w = -OMEGA * (1.0 / diagonal)
+            weight[b] = jnp.broadcast_to(w, (8, BS))
+            g_hi[b, OWN, :], g_lo[b, OWN, :] = split(grouped)
+            l_hi[b], l_lo[b] = split(te_own[b].astype(jnp.float32) + grouped * w)
+
+    def ghost_tables():
+        for p in range(4):
+            @pl.when(exists[p])
+            def _():
+                t_copy(p).wait_recv()
+
+        for p in range(4):
+            def ghost_table(g, c):
+                x = recv_t[p, pl.ds(pl.multiple_of(g * 16, 16), 16), :].astype(jnp.float32)
+                rows = slice((3 - p) * SLAB, (4 - p) * SLAB)
+                te_gh[p * GH + 2 * g, rows, :] = expand(x[0:8], row_agg)
+                te_gh[p * GH + 2 * g + 1, rows, :] = expand(x[8:16], row_agg)
+                return c
+
+            lax.fori_loop(0, GH // 2, ghost_table, 0, unroll=2)
+
+    def ghost_rows(step):
         ghost_copy(step).wait()
-        for u in range(U_GH):
-            b = step * U_GH + u
-            lhs = jnp.concatenate([te_gh[jnp.maximum(slots[b, s] - RB, 0)] for s in range(KO, K)], axis=1)
+        for b in GHOST_GROUPS[step]:
+            lhs = jnp.concatenate(
+                [te_gh[jnp.maximum(slots[b, s] - RB, 0)] for s in range(KO, K)], axis=1
+            )
             rhs = jnp.concatenate([a_v[b, s] for s in range(KO, K)], axis=1)
             ghost = dot(lhs, rhs)
-            own = g_own[b]
-            w = weight[b, 0:1]
-            own_left = te_own[b].astype(jnp.float32) + own * w
-            grouped = jnp.concatenate([ghost[: 2 * SLAB], own, ghost[2 * SLAB :]], axis=0)
-            left = jnp.concatenate([ghost[: 2 * SLAB] * w, own_left, ghost[2 * SLAB :] * w], axis=0)
-            for whole, parts in ((grouped, rights), (left, lefts)):
-                high, low = split(whole)
-                parts[0].append(high)
-                parts[1].append(low)
-        lhs = jnp.concatenate(lefts[0] + lefts[0] + lefts[1], axis=1)
-        rhs = jnp.concatenate(rights[0] + rights[1] + rights[0], axis=1)
-        acc[...] += dot(lhs, rhs)
-        return c
-
-    lax.fori_loop(0, RB // U_GH, ghost_rows, 0)
+            l_gh[b] = (ghost * weight[b, 0:1]).astype(jnp.bfloat16)
+            high, low = split(ghost)
+            for part, whole in ((g_hi, high), (g_lo, low)):
+                part[b, : 2 * SLAB, :] = whole[: 2 * SLAB]
+                part[b, 3 * SLAB :, :] = whole[2 * SLAB :]
+
+    def joined(ref, group):
+        return jnp.concatenate([ref[b] for b in group], axis=1)
+
+    def contract(step):
+        group = GHOST_GROUPS[step]
+        return dot(joined(l_gh, group), joined(g_hi, group))
+
+    for kind, step in ORDER:
+        if kind == "own":
+            own_rows(step)
+            continue
+        if step == 0:
+            ghost_tables()
+        ghost_rows(step)
+        if step == 1:
+            acc[...] = contract(0)
+        elif step > 1:
+            acc[...] += contract(step - 1)
+    last = acc[...] + contract(len(GHOST_GROUPS) - 1)
 
     def c_copy(p):
         return pltpu.make_async_remote_copy(
@@ -191,26 +209,27 @@
             device_id=(me - OFFSETS[p],), device_id_type=MESH,
         )
 
-    for p, o in enumerate(OFFSETS):
-        slab = 2 - o
-        send_c[p, :, 0:SPAN] = acc[slab * SLAB : (slab + 1) * SLAB, :].astype(jnp.bfloat16)
+    for p in range(4):
+        rows = slice((3 - p) * SLAB, (4 - p) * SLAB)
+        send_c[p, :, 0:SPAN] = last[rows].astype(jnp.bfloat16)
         send_c[p, :, SPAN:256] = jnp.zeros((SLAB, 256 - SPAN), jnp.bfloat16)
-    for p in range(4):
+    for p in (0, 3, 1, 2):
         @pl.when(exists[p])
         def _():
             c_copy(p).start()
 
-    lane = lax.broadcasted_iota(jnp.int32, (SLAB, 256), 1)
+    every = range(RB)
+    both = dot(jnp.concatenate([joined(l_hi, every), joined(l_lo, every)], axis=0), joined(g_hi, every))
+    mine = both[:SLAB] + both[SLAB:] + dot(joined(l_hi, every), joined(g_lo, every))
+
     zeros = jnp.zeros((SLAB, 256), jnp.float32)
 
     def placed(x, by):
         wide = jnp.concatenate([x, zeros], axis=1)
         return wide if by == 0 else pltpu.roll(wide, by, 1)
 
-    g_own[0, :, :] = acc[2 * SLAB : 3 * SLAB, 0:128]
-    g_own[1, :, :] = jnp.zeros((SLAB, BS), jnp.float32)
-    g_own[1, :, 0 : SPAN - 128] = acc[2 * SLAB : 3 * SLAB, 128:SPAN]
-    summed = placed(jnp.concatenate([g_own[0], g_own[1]], axis=1), 2 * SLAB)
+    summed = jnp.concatenate([mine, zeros[:, : 256 - SPAN]], axis=1)
+    summed = placed(summed, 2 * SLAB)
     for p, o in enumerate(OFFSETS):
         @pl.when(exists[3 - p])
         def _():
@@ -249,9 +268,13 @@
             pltpu.VMEM((4 * GH, 4 * SLAB, BS), jnp.bfloat16),
             pltpu.VMEM((4, GH * 8, BS), jnp.bfloat16),
             pltpu.VMEM((4, GH * 8, BS), jnp.bfloat16),
-            pltpu.VMEM((RB, SLAB, BS), jnp.float32),
+            pltpu.VMEM((RB, SPAN, BS), jnp.bfloat16),
+            pltpu.VMEM((RB, SPAN, BS), jnp.bfloat16),
+            pltpu.VMEM((RB, SLAB, BS), jnp.bfloat16),
+            pltpu.VMEM((RB, SLAB, BS), jnp.bfloat16),
+            pltpu.VMEM((RB, 4 * SLAB, BS), jnp.bfloat16),
             pltpu.VMEM((RB, 8, BS), jnp.float32),
-            pltpu.VMEM((SPAN, SPAN), jnp.float32),
+            pltpu.VMEM((4 * SLAB, SPAN), jnp.float32),
             pltpu.VMEM((4, SLAB, 256), jnp.bfloat16),
             pltpu.VMEM((4, SLAB, 256), jnp.bfloat16),
             pltpu.VMEM((4, SLAB, BS), jnp.float32),

time: 23 us -> 22.4 us (0.974)
  Pallas kernels: 22.2 us -> 21.6 us
    pallas_call x1, Pallas kernels: 22.2 us -> 21.6 us  [body(): call(matrix_tiles, tentative.transpose(1, 0, 2), column_slots, send_list,...]
where the time goes in v3:
time: 22.4 us; the launch traced here: 22.3 us
  Pallas kernels  21.6 us (96%)
  local copies, waits for them, and re-layouts  0.64 us (3%)
    pallas_call x1, Pallas kernels, body(): call(matrix_tiles, tentative.transpose(1, 0, 2), column_slots, send_list,...  21.6 us
    unnamed x1, local copies, waits for them, and re-layouts  0.64 us

profile of v3, /device:TPU:24, one launch (start us, length us, event | category | flops | bytes accessed | tf_op | source)
XLA Modules:
  0.0 22.3 jit_solution(4335544250299529124)
XLA Ops:
  0.0 21.6 %shard_map.55 = f32[6,8,432]{2,1,0:T(8,128)S(1)} custom-call(bf16[24,27,128,128]{3,2,1,0:T(8,128)(2,1)} %a_hbm.1, bf16[6,24,128]{2,1,0:T(8,128)(2,1)} %bitcast.3, s32[24,27]{1,0:T(8,128)} %slots_hbm.1, s32[1,4,16]{2,1,0:T(4,128)} %send_hbm.1, s32[24,27]{1,0:T(8,128)} %agg_hbm.1), custom_call_target="tpu_custom_call" | custom-call | tf_op jit(solution)/shard_map/pallas_call | solution.py:297
  21.6 0.6 %copy.7 = f32[8,6,432]{2,0,1:T(8,128)} copy(f32[8,6,432]{2,0,1:T(8,128)S(1)} %bitcast.2) | data formatting | bytes 165888

commit v4 on v3

--- a/solution.py
+++ b/solution.py
@@ -30,6 +30,9 @@
 GHOST_GROUPS = groups(8, 8, 8)
 ORDER = [("own", 0), ("own", 1), ("own", 2), ("own", 3), ("own", 4), ("own", 5), ("ghost", 0), ("ghost", 1), ("ghost", 2)]
 AHEAD = 2
+GHOST_STREAMED = 4
+PARTS = 3
+GREET = 1
 STREAMED = 8
 MESH = pl.DeviceIdType.MESH
 
@@ -114,19 +117,20 @@
 
     lax.fori_loop(0, RB, own_table, 0, unroll=4)
 
-    total = sum(e.astype(jnp.int32) for e in exists)
-    pl.semaphore_wait(barrier, total)
-
     def t_copy(p):
         return pltpu.make_async_remote_copy(
             src_ref=send_t.at[p], dst_ref=recv_t.at[p], send_sem=st_sem.at[p], recv_sem=rt_sem.at[p],
             device_id=(me + OFFSETS[p],), device_id_type=MESH,
         )
 
-    for p in range(4):
-        @pl.when(exists[3 - p])
-        def _():
-            t_copy(p).start()
+    def send_blocks():
+        total = sum(e.astype(jnp.int32) for e in exists)
+        pl.semaphore_wait(barrier, total)
+
+        for p in range(4):
+            @pl.when(exists[3 - p])
+            def _():
+                t_copy(p).start()
 
     def zero_table(v, c):
         te_gh[v] = jnp.zeros((4 * SLAB, BS), jnp.bfloat16)
@@ -153,30 +157,31 @@
             g_hi[b, OWN, :], g_lo[b, OWN, :] = split(grouped)
             l_hi[b], l_lo[b] = split(te_own[b].astype(jnp.float32) + grouped * w)
 
-    def ghost_tables():
-        for p in range(4):
-            @pl.when(exists[p])
-            def _():
-                t_copy(p).wait_recv()
-
-        for p in range(4):
-            def ghost_table(g, c):
-                x = recv_t[p, pl.ds(pl.multiple_of(g * 16, 16), 16), :].astype(jnp.float32)
-                rows = slice((3 - p) * SLAB, (4 - p) * SLAB)
-                te_gh[p * GH + 2 * g, rows, :] = expand(x[0:8], row_agg)
-                te_gh[p * GH + 2 * g + 1, rows, :] = expand(x[8:16], row_agg)
-                return c
-
-            lax.fori_loop(0, GH // 2, ghost_table, 0, unroll=2)
+    def ghost_tables(p):
+        @pl.when(exists[p])
+        def _():
+            t_copy(p).wait_recv()
+
+        def ghost_table(g, c):
+            x = recv_t[p, pl.ds(pl.multiple_of(g * 16, 16), 16), :].astype(jnp.float32)
+            rows = slice((3 - p) * SLAB, (4 - p) * SLAB)
+            te_gh[p * GH + 2 * g, rows, :] = expand(x[0:8], row_agg)
+            te_gh[p * GH + 2 * g + 1, rows, :] = expand(x[8:16], row_agg)
+            return c
+
+        lax.fori_loop(0, GH // 2, ghost_table, 0, unroll=8)
 
     def ghost_rows(step):
-        ghost_copy(step).wait()
+        if step % PARTS == 0:
+            for later in range(step, min(step + PARTS, len(GHOST_GROUPS))):
+                ghost_copy(later).wait()
         for b in GHOST_GROUPS[step]:
-            lhs = jnp.concatenate(
-                [te_gh[jnp.maximum(slots[b, s] - RB, 0)] for s in range(KO, K)], axis=1
-            )
-            rhs = jnp.concatenate([a_v[b, s] for s in range(KO, K)], axis=1)
-            ghost = dot(lhs, rhs)
+            table = [te_gh[jnp.maximum(slots[b, s] - RB, 0)] for s in range(KO, K)]
+            tile = [a_v[b, s] for s in range(KO, K)]
+            cut = KG - GHOST_STREAMED
+            ghost = dot(jnp.concatenate(table[:cut], axis=1), jnp.concatenate(tile[:cut], axis=1))
+            if GHOST_STREAMED:
+                ghost = ghost + dot(jnp.concatenate(tile[cut:], axis=1), jnp.concatenate(table[cut:], axis=1)).T
             l_gh[b] = (ghost * weight[b, 0:1]).astype(jnp.bfloat16)
             high, low = split(ghost)
             for part, whole in ((g_hi, high), (g_lo, low)):
@@ -192,10 +197,13 @@
 
     for kind, step in ORDER:
         if kind == "own":
+            if step == GREET:
+                send_blocks()
             own_rows(step)
             continue
         if step == 0:
-            ghost_tables()
+            for p in (2, 3, 1, 0):
+                ghost_tables(p)
         ghost_rows(step)
         if step == 1:
             acc[...] = contract(0)
@@ -213,7 +221,7 @@
         rows = slice((3 - p) * SLAB, (4 - p) * SLAB)
         send_c[p, :, 0:SPAN] = last[rows].astype(jnp.bfloat16)
         send_c[p, :, SPAN:256] = jnp.zeros((SLAB, 256 - SPAN), jnp.bfloat16)
-    for p in (0, 3, 1, 2):
+    for p in (0, 1, 3, 2):
         @pl.when(exists[p])
         def _():
             c_copy(p).start()
@@ -230,12 +238,12 @@
 
     summed = jnp.concatenate([mine, zeros[:, : 256 - SPAN]], axis=1)
     summed = placed(summed, 2 * SLAB)
-    for p, o in enumerate(OFFSETS):
+    for p in (2, 3, 1, 0):
         @pl.when(exists[3 - p])
         def _():
             c_copy(p).wait_recv()
-    for p, o in enumerate(OFFSETS):
-        summed = summed + placed(recv_c[p].astype(jnp.float32), (o + 2) * SLAB)
+
+        summed = summed + placed(recv_c[p].astype(jnp.float32), (OFFSETS[p] + 2) * SLAB)
     for t in range(4):
         result[t] = summed[:, t * BS : (t + 1) * BS]
     for m in range(MODES):

time: 22.4 us -> 21.8 us (0.973)
  Pallas kernels: 21.6 us -> 21 us
    pallas_call x1, Pallas kernels: 21.6 us -> 21 us  [body(): call(matrix_tiles, tentative.transpose(1, 0, 2), column_slots, send_list,...]
where the time goes in v4:
time: 21.8 us; the launch traced here: 21.7 us
  Pallas kernels  21 us (96%)
  local copies, waits for them, and re-layouts  0.64 us (3%)
    pallas_call x1, Pallas kernels, body(): call(matrix_tiles, tentative.transpose(1, 0, 2), column_slots, send_list,...  21 us
    unnamed x1, local copies, waits for them, and re-layouts  0.64 us

profile of v4, /device:TPU:24, one launch (start us, length us, event | category | flops | bytes accessed | tf_op | source)
XLA Modules:
  0.0 21.7 jit_solution(10497113641590369884)
XLA Ops:
  0.0 21.0 %shard_map.55 = f32[6,8,432]{2,1,0:T(8,128)S(1)} custom-call(bf16[24,27,128,128]{3,2,1,0:T(8,128)(2,1)} %a_hbm.1, bf16[6,24,128]{2,1,0:T(8,128)(2,1)} %bitcast.3, s32[24,27]{1,0:T(8,128)} %slots_hbm.1, s32[1,4,16]{2,1,0:T(4,128)} %send_hbm.1, s32[24,27]{1,0:T(8,128)} %agg_hbm.1), custom_call_target="tpu_custom_call" | custom-call | tf_op jit(solution)/shard_map/pallas_call | solution.py:305
  21.0 0.6 %copy.7 = f32[8,6,432]{2,0,1:T(8,128)} copy(f32[8,6,432]{2,0,1:T(8,128)S(1)} %bitcast.2) | data formatting | bytes 165888

commit v5 on v4

--- a/solution.py
+++ b/solution.py
@@ -63,6 +63,15 @@
     a_sem, small_sem, st_sem, rt_sem, sc_sem, rc_sem,
 ):
     me = lax.axis_index("dom")
+    exists = [jnp.logical_and(me - o >= 0, me - o < count) for o in OFFSETS]
+    recv_c[...] = jnp.zeros_like(recv_c)
+    send_c[:, :, SPAN:256] = jnp.zeros((4, SLAB, 256 - SPAN), jnp.bfloat16)
+    barrier = pltpu.get_barrier_semaphore()
+    for p, o in enumerate(OFFSETS):
+        @pl.when(exists[p])
+        def _():
+            pl.semaphore_signal(barrier, inc=1, device_id=(me - o,), device_id_type=MESH)
+
     small = [
         pltpu.make_async_copy(src, dst, small_sem.at[i])
         for i, (src, dst) in enumerate(
@@ -82,14 +91,6 @@
         part = (pl.ds(group.start, len(group)), pl.ds(KO, KG))
         return pltpu.make_async_copy(a_hbm.at[part], a_v.at[part], a_sem.at[1, step])
 
-
-    exists = [jnp.logical_and(me - o >= 0, me - o < count) for o in OFFSETS]
-    recv_c[...] = jnp.zeros_like(recv_c)
-    barrier = pltpu.get_barrier_semaphore()
-    for p, o in enumerate(OFFSETS):
-        @pl.when(exists[p])
-        def _():
-            pl.semaphore_signal(barrier, inc=1, device_id=(me - o,), device_id_type=MESH)
 
     for kind, step in ORDER[:AHEAD]:
         (own_copy if kind == "own" else ghost_copy)(step).start()
@@ -217,10 +218,9 @@
             device_id=(me - OFFSETS[p],), device_id_type=MESH,
         )
 
-    for p in range(4):
+    for p in (0, 1, 3, 2):
         rows = slice((3 - p) * SLAB, (4 - p) * SLAB)
         send_c[p, :, 0:SPAN] = last[rows].astype(jnp.bfloat16)
-        send_c[p, :, SPAN:256] = jnp.zeros((SLAB, 256 - SPAN), jnp.bfloat16)
     for p in (0, 1, 3, 2):
         @pl.when(exists[p])
         def _():

time: 21.8 us -> 21.8 us (level)
  no operation moved by 1% of the time
where the time goes in v5:
time: 21.8 us; the launch traced here: 21.7 us
  Pallas kernels  21 us (96%)
  local copies, waits for them, and re-layouts  0.64 us (3%)
    pallas_call x1, Pallas kernels, body(): call(matrix_tiles, tentative.transpose(1, 0, 2), column_slots, send_list,...  21 us
    unnamed x1, local copies, waits for them, and re-layouts  0.64 us

profile of v5, /device:TPU:24, one launch (start us, length us, event | category | flops | bytes accessed | tf_op | source)
XLA Modules:
  0.0 21.7 jit_solution(4500878326273988938)
XLA Ops:
  0.0 21.0 %shard_map.55 = f32[6,8,432]{2,1,0:T(8,128)S(1)} custom-call(bf16[24,27,128,128]{3,2,1,0:T(8,128)(2,1)} %a_hbm.1, bf16[6,24,128]{2,1,0:T(8,128)(2,1)} %bitcast.3, s32[24,27]{1,0:T(8,128)} %slots_hbm.1, s32[1,4,16]{2,1,0:T(4,128)} %send_hbm.1, s32[24,27]{1,0:T(8,128)} %agg_hbm.1), custom_call_target="tpu_custom_call" | custom-call | tf_op jit(solution)/shard_map/pallas_call | solution.py:305
  21.0 0.6 %copy.7 = f32[8,6,432]{2,0,1:T(8,128)} copy(f32[8,6,432]{2,0,1:T(8,128)S(1)} %bitcast.2) | data formatting | bytes 165888
